TPU v7x, 256 devices: a whole 4x4x8 slice. The times are simulated.
256 devices in a mesh: row: 32 (over x, y, core), col: 8 (over z).
Axes of the slice: x: 4, y: 4, z: 8, core: 2. Of those that a mesh axis runs over, the one named last changes fastest.
Arguments:
- blocks: float32 [32, 8, 8, 32, 2, 8, 128], P('row', 'col'), may hold values from 0.5 to 1620
- plan: int32 [32, 8, 8, 32, 2], P('row', 'col'), may hold values from 0 to 4095, as said below
- live: int32 [32, 8, 8, 32], P('row', 'col'), may hold values from 1 to 2, as said below
- row_emb: float32 [300, 32768], P(None, ('row', 'col')), may hold values from -1.5 to 1.5
- col_emb: float32 [300, 32768], P(None, ('col', 'row')), may hold values from -1.5 to 1.5
- row_acc: float32 [300, 32768], P(None, ('row', 'col')), may hold values from 0.5 to 5
- col_acc: float32 [300, 32768], P(None, ('col', 'row')), may hold values from 0.5 to 5
Outputs:
- new_row_emb: float32 [300, 32768], P(None, ('row', 'col'))
- new_col_emb: float32 [300, 32768], P(None, ('col', 'row'))
- new_row_acc: float32 [300, 32768], P(None, ('row', 'col'))
- new_col_acc: float32 [300, 32768], P(None, ('col', 'row'))
Inputs may be any that keep to these rules, and one draw needn't show every extreme that they name: plan[r, c, c2, r2, p] is a sub-block number of tile (r, c); numbers may repeat and repeated slots add. Over all index pairs (r2, c2), slot 0 names every sub-block row and every sub-block column of each tile. Slots at or past live[r, c, c2, r2] hold values that are not counts. In every draw some tile gets 2 live slots from every index pair.
All inputs are finite; a program needn't handle non-finite values.
Results may differ from a plain program's by a relative error of at most 0.0003.
Values sent between devices are 32-bit elements; how exact they have to be, the bound alone decides.
No kernel may reach another device: no remote copies, remote signals or barrier semaphores. Data moves between devices by JAX's collectives and lax.ppermute only.
A program may use at most 192 MiB of HBM per device.

v0:
```python
import jax
import jax.numpy as jnp
from jax import lax
from jax.sharding import PartitionSpec as P

LEARNING_RATE = 0.2


def per_device(blocks, plan, live, row_emb, col_emb, row_acc, col_acc):
    rows_count = lax.axis_size("row")
    cols_count = lax.axis_size("col")
    highest = lax.Precision.HIGHEST
    outgoing = blocks[0, 0]
    arrived = lax.all_to_all(
        lax.all_to_all(outgoing, "row", split_axis=1, concat_axis=1, tiled=True),
        "col",
        split_axis=0,
        concat_axis=0,
        tiled=True,
    )
    sub_rows = blocks.shape[5]
    sub_cols = blocks.shape[6]
    tile_rows = row_emb.shape[1] * cols_count
    tile_cols = col_emb.shape[1] * rows_count
    grid_row_count = tile_rows // sub_rows
    grid_column_count = tile_cols // sub_cols
    block_total = grid_row_count * grid_column_count
    places = plan[0, 0]
    limits = live[0, 0]
    slot_ids = lax.broadcasted_iota(jnp.int32, places.shape, 2)
    target = jnp.where(slot_ids < limits[:, :, None], places, block_total)
    flat_layout = arrived.reshape(-1, sub_rows * sub_cols)
    dense_block_matrix = jax.ops.segment_sum(
        flat_layout, target.reshape(-1), num_segments=block_total + 1
    )[:block_total]
    tile_counts = (
        dense_block_matrix.reshape(grid_row_count, grid_column_count, sub_rows, sub_cols)
        .transpose(0, 2, 1, 3)
        .reshape(tile_rows, tile_cols)
    )
    row_part = jnp.sum(tile_counts, axis=1)
    col_part = jnp.sum(tile_counts, axis=0)
    col_mass = lax.psum(col_part, "row")
    row_mass = lax.psum(row_part, "col")
    grand_total = lax.psum(jnp.sum(row_part), ("row", "col"))
    row_block = lax.all_gather(row_emb, "col", axis=1, tiled=True)
    col_block = lax.all_gather(col_emb, "row", axis=1, tiled=True)
    rows_all = tile_rows * rows_count
    cols_all = tile_cols * cols_count
    loss_scale = 4.0 * float(rows_all * cols_all) ** (-0.25)
    col_base = jnp.log(grand_total) - jnp.log(col_mass)[None, :]
    row_logs = jnp.log(row_mass)
    step_rows = min(512, tile_rows)
    col_term = jnp.zeros((col_block.shape[0], tile_cols), jnp.float32)
    row_pieces = []
    for start in range(0, tile_rows, step_rows):
        counts_part = tile_counts[start : start + step_rows]
        vectors_part = row_block[:, start : start + step_rows]
        scores = lax.dot_general(
            vectors_part, col_block, (((0,), (0,)), ((), ())), precision=highest
        )
        baseline = col_base - row_logs[start : start + step_rows][:, None]
        positive = counts_part > 0
        pmi_target = jnp.log(jnp.where(positive, counts_part, 1.0)) + baseline
        confidence = 0.1 + 0.25 * jnp.sqrt(counts_part)
        loss_grad = (
            jnp.where(
                positive, confidence * (scores - pmi_target), jax.nn.sigmoid(scores - baseline)
            )
            * loss_scale
        )
        row_pieces.append(
            lax.dot_general(col_block, loss_grad, (((1,), (1,)), ((), ())), precision=highest)
        )
        col_term = col_term + jnp.dot(vectors_part, loss_grad, precision=highest)
    row_term = jnp.concatenate(row_pieces, axis=1)
    row_share = lax.psum_scatter(row_term, "col", scatter_dimension=1, tiled=True)
    col_share = lax.psum_scatter(col_term, "row", scatter_dimension=1, tiled=True)
    new_row_acc = row_acc + row_share * row_share
    new_col_acc = col_acc + col_share * col_share
    new_row_emb = row_emb - LEARNING_RATE * row_share / jnp.sqrt(new_row_acc)
    new_col_emb = col_emb - LEARNING_RATE * col_share / jnp.sqrt(new_col_acc)
    return (new_row_emb, new_col_emb, new_row_acc, new_col_acc)


def solution(mesh):
    return jax.shard_map(
        per_device,
        mesh=mesh,
        in_specs=(
            P("row", "col", None, None, None, None, None),
            P("row", "col", None, None, None),
            P("row", "col", None, None),
            P(None, ("row", "col")),
            P(None, ("col", "row")),
            P(None, ("row", "col")),
            P(None, ("col", "row")),
        ),
        out_specs=(
            P(None, ("row", "col")),
            P(None, ("col", "row")),
            P(None, ("row", "col")),
            P(None, ("col", "row")),
        ),
        check_vma=False,
    )
```

profile of v0, /device:TPU:2, one launch (start us, length us, event | category | flops | bytes accessed | tf_op | source)
XLA Modules:
  0.0 581.3 jit_solution(6106549809527180893)
XLA Ops:
  7.2 0.0 all-gather.3.cloned.1.call-start
  7.2 0.7 all-gather.3.cloned.1.call-update
  7.9 0.0 all-gather.5.cloned.1.call-start
  7.9 0.7 all-gather.5.cloned.1.call-update
  8.7 0.0 copy-start.9
  8.7 0.0 copy-start.8
  8.7 1.8 copy.27
  10.5 33.1 %all_to_all.10 = f32[8,32,2,8,128]{4,3,2,0,1:T(8,128)S(1)} all-to-all(f32[8,32,2,8,128]{4,3,2,0,1:T(8,128)S(1)} %bitcast.54), channel_id=1, replica_groups=mesh['row'=32,'col'=8] {'row'}, dimensions={1} | all-to-all | bytes 4194304 | tf_op jit(solution)/shard_map/all_to_all | solution.py:15
  43.6 1.5 copy.19
  45.1 8.5 %all-to-all-start.1 = ((f32[8,32,2,8,128]{4,3,2,1,0:T(8,128)}), f32[8,32,2,8,128]{4,3,2,1,0:T(8,128)S(1)}, u32[]{:S(2)}, u32[]{:S(2)}) async-start(f32[8,32,2,8,128]{4,3,2,1,0:T(8,128)} %copy.19), calls=%async_computation.1 | async-start | bytes 4194304 | tf_op jit(solution)/shard_map/all_to_all | solution.py:14
  53.6 0.0 reduce-scatter.3.cloned.1.call-start
  53.6 0.0 copy-done.9
  53.7 0.1 iota_compare_fusion
  53.8 0.1 lt.23
  53.9 0.0 copy-done.8
  53.9 0.1 copy.17
  54.1 0.1 squeeze.6
  54.2 51.8 %all-to-all-done.1 = f32[8,32,2,8,128]{4,3,2,1,0:T(8,128)S(1)} async-done(((f32[8,32,2,8,128]{4,3,2,1,0:T(8,128)}), f32[8,32,2,8,128]{4,3,2,1,0:T(8,128)S(1)}, u32[]{:S(2)}, u32[]{:S(2)}) %all-to-all-start.1) | async-done | bytes 2097184 | tf_op jit(solution)/shard_map/all_to_all | solution.py:14
  106.0 11.9 %scatter_custom_fusion = f32[4097,1024]{1,0:T(8,128)} fusion(s32[512]{0:T(512)S(1)} %bitcast.58, f32[]{:T(128)} %constant.7.clone.1, f32[64,8,8,128]{3,2,1,0:T(8,128)S(1)} %bitcast.55), kind=kCustom, calls=%fused_computation.12 | custom fusion | flops 524288 | bytes 18878468 | tf_op jit(solution)/shard_map/scatter-add | solution.py:33
  117.9 13.3 %slice_reduce_fusion = (f32[]{:T(128)}, f32[512,8,8,128]{3,1,2,0:T(8,128)}) fusion(f32[4097,1024]{1,0:T(8,128)} %scatter_custom_fusion), kind=kLoop, calls=%fused_computation.2 | loop fusion | flops 4194303 | bytes 33554436 | tf_op jit(solution)/shard_map/reduce_sum | solution.py:45
  131.2 72.8 %psum.21 = f32[]{:T(128)} all-reduce(f32[]{:T(128)} %get-tuple-element.10), channel_id=1, replica_groups=mesh['row'=32,'col'=8] {'row','col'}, use_global_device_ids=true, to_apply=%region_2.3 | all-reduce | flops 1 | bytes 8 | tf_op jit(solution)/shard_map/psum | solution.py:45
  204.7 14.3 %copy.21 = f32[512,8,8,128]{3,2,1,0:T(8,128)} copy(f32[512,8,8,128]{3,1,2,0:T(8,128)} %get-tuple-element.11) | data formatting | bytes 33554432
  218.9 7.2 %fusion.27 = (f32[32,128]{1,0:T(8,128)S(1)}, f32[128,8]{1,0:T(8,128)S(1)}) fusion(f32[128,32,8,128]{3,2,1,0:T(8,128)} %bitcast.52), kind=kLoop, calls=%fused_computation.53 | loop fusion | flops 8383488 | bytes 16797696 | tf_op jit(solution)/shard_map/reduce_sum | solution.py:42
  226.1 0.1 reduce_sum.35
  226.2 16.2 %psum.23 = f32[1024]{0:T(1024)S(1)} all-reduce(f32[1024]{0:T(1024)S(1)} %reduce_sum.35), channel_id=1, replica_groups=mesh['row'=32,'col'=8] {'col'}, use_global_device_ids=true, to_apply=%region_6.7 | all-reduce | flops 1024 | bytes 8192 | tf_op jit(solution)/shard_map/psum | solution.py:44
  242.5 107.5 %psum.22 = f32[4096]{0:T(1024)S(1)} all-reduce(f32[4096]{0:T(1024)S(1)} %bitcast.56), channel_id=1, replica_groups=mesh['row'=32,'col'=8] {'row'}, use_global_device_ids=true, to_apply=%region_4.5 | all-reduce | flops 4096 | bytes 32768 | tf_op jit(solution)/shard_map/psum | solution.py:43
  350.0 11.7 %bitcast_bitcast_fusion = f32[128,8,32,128]{3,1,2,0:T(8,128)} fusion(f32[128,32,8,128]{3,2,1,0:T(8,128)} %bitcast.53), kind=kLoop, calls=%fused_computation.1 | loop fusion | bytes 33554432 | tf_op jit(solution)/shard_map/transpose | solution.py:38
  361.6 0.0 all-gather.3.cloned.1.call-done
  361.6 0.0 all-gather.5.cloned.1.call-done
  361.6 0.0 copy-start.2
  361.6 0.0 copy-start.3
  361.7 21.9 %fusion.5 = f32[512,4096]{1,0:T(8,128)S(1)} fusion(f32[128,8,32,128]{3,1,2,0:T(8,128)} %bitcast_bitcast_fusion, f32[512]{0:T(512)S(1)} %get-tuple-element.13, f32[4096]{0:T(1024)S(1)} %log_subtract_fusion, f32[300,4096]{1,0:T(8,128)} %all-gather.5.cloned.1.call-done, f32[300,1024]{1,0:T(8,128)} %all-gather.3.cloned.1.call-done), kind=kOutput, calls=%fused_computation.17 | convolution fusion | flops 7579107328 | bytes 22398976 | tf_op jit(solution)/shard_map/dot_general | solution.py:59
  383.6 0.0 copy-start
  383.6 0.0 copy-done.2
  383.6 0.0 copy-done.3
  383.6 25.7 %fusion.3 = f32[512,4096]{1,0:T(8,128)S(1)} fusion(f32[128,8,32,128]{3,1,2,0:T(8,128)} %bitcast_bitcast_fusion, f32[512]{0:T(512)S(1)} %get-tuple-element.12, f32[4096]{0:T(1024)S(1)} %log_subtract_fusion, f32[300,4096]{1,0:T(8,128)S(1)} %copy-done.2, f32[300,1024]{1,0:T(8,128)S(1)} %copy-done.3), kind=kOutput, calls=%fused_computation.15 | convolution fusion | flops 7579107328 | bytes 22398976 | tf_op jit(solution)/shard_map/dot_general | solution.py:59
  409.3 0.0 copy-start.1
  409.3 8.6 %convolution_bitcast_fusion.1 = f32[300,512]{1,0:T(8,128)S(1)} fusion(f32[512,4096]{1,0:T(8,128)S(1)} %fusion.3, f32[300,4096]{1,0:T(8,128)S(1)} %copy-done.2), kind=kOutput, calls=%fused_computation.38 | convolution fusion | flops 7549747200 | bytes 13918208 | tf_op jit(solution)/shard_map/dot_general | solution.py:73
  417.9 0.0 copy-done
  417.9 0.0 copy-done.1
  417.9 8.8 %convolution_bitcast_fusion = f32[300,512]{1,0:T(8,128)S(1)} fusion(f32[512,4096]{1,0:T(8,128)S(1)} %fusion.5, f32[300,4096]{1,0:T(8,128)S(1)} %copy-done.2), kind=kOutput, calls=%fused_computation.37 | convolution fusion | flops 7549747200 | bytes 13918208 | tf_op jit(solution)/shard_map/dot_general | solution.py:73
  426.7 1.1 pad_maximum_fusion
  427.9 0.0 reduce-scatter.3.cloned.1.call-update
  427.9 0.0 reduce-scatter.5.cloned.1.call-start
  428.0 11.3 %fusion.23 = f32[4096,300]{0,1:T(8,128)S(1)} fusion(f32[512,4096]{1,0:T(8,128)} %copy-done.1, f32[300,1024]{1,0:T(8,128)S(1)} %copy-done.3), kind=kOutput, calls=%fused_computation.42 | convolution fusion | flops 7549747200 | bytes 13926400 | tf_op jit(solution)/shard_map/dot_general | solution.py:75
  439.2 0.0 copy-start.4
  439.2 0.0 copy-start.6
  439.2 0.0 copy-start.5
  439.3 0.0 copy-start.7
  439.3 12.8 %fusion.18 = f32[300,4096]{1,0:T(8,128)} fusion(f32[4096,300]{0,1:T(8,128)S(1)} %fusion.23, f32[512,4096]{1,0:T(8,128)} %copy-done, f32[300,1024]{1,0:T(8,128)S(1)} %copy-done.3), kind=kOutput, calls=%fused_computation.33 | convolution fusion | flops 7550976000 | bytes 18907136 | tf_op jit(solution)/shard_map/dot_general | solution.py:75
  452.1 0.0 reduce-scatter.5.cloned.1.call-update
  452.1 25.8 %reduce-scatter.3.cloned.1.call-done = f32[300,128]{1,0:T(8,128)} async-done(((f32[300,1024]{1,0:T(8,128)}), f32[300,128]{1,0:T(8,128)}) %reduce-scatter.3.cloned.1.call-update) | async-done | bytes 153616 | tf_op jit(solution)/shard_map/reduce_scatter | solution.py:77
  477.9 0.0 copy-done.4
  477.9 0.0 copy-done.6
  477.9 1.7 multiply_subtract_fusion.1
  479.6 93.4 %reduce-scatter.5.cloned.1.call-done = f32[300,128]{1,0:T(8,128)} async-done(((f32[300,4096]{1,0:T(8,128)}), f32[300,128]{1,0:T(8,128)}) %reduce-scatter.5.cloned.1.call-update) | async-done | bytes 153616 | tf_op jit(solution)/shard_map/reduce_scatter | solution.py:78
  572.9 0.0 copy-done.5
  572.9 0.0 copy-done.7
  572.9 1.7 multiply_subtract_fusion
  (4 shorter events, 0.0 us)
Async XLA Ops:
  7.2 354.5 %all-gather.3.cloned.1.call-start = ((), (), s32[]{:S(2)}) async-start(), calls=%async_computation.4 | async-start | bytes 1400832 | tf_op jit(solution)/shard_map/all_gather | solution.py:46
  7.9 353.7 %all-gather.5.cloned.1.call-start = ((), (), s32[]{:S(2)}) async-start(), calls=%async_computation.5 | async-start | bytes 5136384 | tf_op jit(solution)/shard_map/all_gather | solution.py:47
  8.7 45.0 %copy-start.9 = (s32[1,1,8,32]{3,2,1,0:T(8,128)S(1)}, s32[1,1,8,32]{3,2,1,0:T(8,128)}, u32[]{:S(2)}) copy-start(s32[1,1,8,32]{3,2,1,0:T(8,128)} %param.9) | copy-start | bytes 3076
  8.7 45.3 %copy-start.8 = (s32[1,1,8,32,2]{3,4,2,1,0:T(2,128)S(1)}, s32[1,1,8,32,2]{3,4,2,1,0:T(2,128)}, u32[]{:S(2)}) copy-start(s32[1,1,8,32,2]{3,4,2,1,0:T(2,128)} %param.8) | copy-start | bytes 6148
  45.1 60.9 %all-to-all-start.1 = ((f32[8,32,2,8,128]{4,3,2,1,0:T(8,128)}), f32[8,32,2,8,128]{4,3,2,1,0:T(8,128)S(1)}, u32[]{:S(2)}, u32[]{:S(2)}) async-start(f32[8,32,2,8,128]{4,3,2,1,0:T(8,128)} %copy.19), calls=%async_computation.1 | async-start | bytes 4194304 | tf_op jit(solution)/shard_map/all_to_all | solution.py:14
  53.6 424.3 %reduce-scatter.3.cloned.1.call-start = ((), (), s32[]{:S(2)}) async-start(), calls=%async_computation.6 | async-start | bytes 1400832 | tf_op jit(solution)/shard_map/reduce_scatter | solution.py:77
  361.6 22.0 %copy-start.2 = (f32[300,4096]{1,0:T(8,128)S(1)}, f32[300,4096]{1,0:T(8,128)}, u32[]{:S(2)}) copy-start(f32[300,4096]{1,0:T(8,128)} %all-gather.5.cloned.1.call-done) | copy-start | bytes 14745604
  361.6 22.0 %copy-start.3 = (f32[300,1024]{1,0:T(8,128)S(1)}, f32[300,1024]{1,0:T(8,128)}, u32[]{:S(2)}) copy-start(f32[300,1024]{1,0:T(8,128)} %all-gather.3.cloned.1.call-done) | copy-start | bytes 3686404
  383.6 34.3 %copy-start = (f32[512,4096]{1,0:T(8,128)}, f32[512,4096]{1,0:T(8,128)S(1)}, u32[]{:S(2)}) copy-start(f32[512,4096]{1,0:T(8,128)S(1)} %fusion.5) | copy-start | bytes 25165828
  409.3 8.6 %copy-start.1 = (f32[512,4096]{1,0:T(8,128)}, f32[512,4096]{1,0:T(8,128)S(1)}, u32[]{:S(2)}) copy-start(f32[512,4096]{1,0:T(8,128)S(1)} %fusion.3) | copy-start | bytes 25165828
  427.9 145.0 %reduce-scatter.5.cloned.1.call-start = ((), (), s32[]{:S(2)}) async-start(), calls=%async_computation.7 | async-start | bytes 5136384 | tf_op jit(solution)/shard_map/reduce_scatter | solution.py:78
  439.2 38.7 %copy-start.4 = (f32[300,128]{1,0:T(8,128)S(1)}, f32[300,128]{1,0:T(8,128)}, u32[]{:S(2)}) copy-start(f32[300,128]{1,0:T(8,128)} %param.10) | copy-start | bytes 460804
  439.2 38.7 %copy-start.6 = (f32[300,128]{1,0:T(8,128)S(1)}, f32[300,128]{1,0:T(8,128)}, u32[]{:S(2)}) copy-start(f32[300,128]{1,0:T(8,128)} %param.12) | copy-start | bytes 460804
  439.2 133.7 %copy-start.5 = (f32[300,128]{1,0:T(8,128)S(1)}, f32[300,128]{1,0:T(8,128)}, u32[]{:S(2)}) copy-start(f32[300,128]{1,0:T(8,128)} %param.11) | copy-start | bytes 460804
  439.3 133.7 %copy-start.7 = (f32[300,128]{1,0:T(8,128)S(1)}, f32[300,128]{1,0:T(8,128)}, u32[]{:S(2)}) copy-start(f32[300,128]{1,0:T(8,128)} %param.13) | copy-start | bytes 460804
Sparse Core Ops, SparseCore 0:
  9.7 44.0 all-gather.2
  56.2 54.9 all-gather.4
  428.0 49.8 reduce-scatter.2
  481.9 91.0 reduce-scatter.4
where the time goes:
time: 589 us; the launch traced here: 581 us
  blocking collectives  230 us (39%)
  waiting for transfers between devices  172 us (29%)
  matrix products  89 us (15%)
  other arithmetic  37 us (6%)
  local copies, waits for them, and re-layouts  29.9 us (5%)
  between operations  14.8 us (3%)
  starting transfers between devices  8.62 us (1%)
    psum x1, blocking collectives, per_device(): col_mass = lax.psum(col_part, 'row')  107 us
    reduce_scatter x1, waiting for transfers between devices, per_device(): lax.psum_scatter(col_term, 'row', scatter_dimension=1, tiled=True)  93.4 us
    psum x1, blocking collectives, per_device(): grand_total = lax.psum(jnp.sum(row_part), ('row', 'col'))  72.8 us
    all_to_all x1, waiting for transfers between devices, per_device(): lax.all_to_all(lax.all_to_all(outgoing, 'row', split_axis=1, concat_axis=...  51.8 us
    dot_general x2, matrix products, per_device(): lax.dot_general(vectors_part, col_block, (((0,), (0,)), ((), ())), precis...  47.6 us
    all_to_all x1, blocking collectives, per_device(): lax.all_to_all(outgoing, 'row', split_axis=1, concat_axis=1, tiled=True)  33.1 us
    reduce_scatter x1, waiting for transfers between devices, per_device(): lax.psum_scatter(row_term, 'col', scatter_dimension=1, tiled=True)  25.8 us
    dot_general x2, matrix products, per_device(): col_term = col_term + jnp.dot(vectors_part, loss_grad, precision=highest)  24.1 us
  transfers between devices with their start and end apart: 5, of which 3 were waited for; matrix products, arithmetic and copies ran while one was open for 15% of the time, Pallas kernels for 0%

commit v1 on v0

--- a/solution.py
+++ b/solution.py
@@ -40,7 +40,7 @@
     )
     row_part = jnp.sum(tile_counts, axis=1)
     col_part = jnp.sum(tile_counts, axis=0)
-    col_mass = lax.psum(col_part, "row")
+    col_mass = jnp.sum(lax.all_gather(col_part, "row"), axis=0)
     row_mass = lax.psum(row_part, "col")
     grand_total = lax.psum(jnp.sum(row_part), ("row", "col"))
     row_block = lax.all_gather(row_emb, "col", axis=1, tiled=True)

time: 589 us -> 491 us (0.83)
  blocking collectives: 230 us -> 146 us
  waiting for transfers between devices: 172 us -> 158 us
    psum x1 -> x0, blocking collectives: 107 us -> none  [per_device(): col_mass = lax.psum(col_part, 'row')]
    all_gather x0 -> x1, blocking collectives: none -> 23.7 us  [per_device(): col_mass = jnp.sum(lax.all_gather(col_part, 'row'), axis=0)]
    reduce_scatter x1, waiting for transfers between devices: 25.8 us -> 11.2 us  [per_device(): lax.psum_scatter(row_term, 'col', scatter_dimension=1, tiled=True)]
  transfers between devices with their start and end apart: 5 -> 5, of which waited for: 3 -> 3; matrix products, arithmetic and copies ran while one was open for 15% -> 18% of each run, Pallas kernels for 0% -> 0%
where the time goes in v1:
time: 491 us; the launch traced here: 483 us
  waiting for transfers between devices  158 us (32%)
  blocking collectives  146 us (30%)
  matrix products  89.1 us (18%)
  other arithmetic  37.4 us (8%)
  local copies, waits for them, and re-layouts  29.9 us (6%)
  between operations  14.9 us (3%)
  starting transfers between devices  8.62 us (2%)
    reduce_scatter x1, waiting for transfers between devices, per_device(): lax.psum_scatter(col_term, 'row', scatter_dimension=1, tiled=True)  93.3 us
    psum x1, blocking collectives, per_device(): grand_total = lax.psum(jnp.sum(row_part), ('row', 'col'))  72.8 us
    all_to_all x1, waiting for transfers between devices, per_device(): lax.all_to_all(lax.all_to_all(outgoing, 'row', split_axis=1, concat_axis=...  51.8 us
    dot_general x2, matrix products, per_device(): lax.dot_general(vectors_part, col_block, (((0,), (0,)), ((), ())), precis...  47.6 us
    all_to_all x1, blocking collectives, per_device(): lax.all_to_all(outgoing, 'row', split_axis=1, concat_axis=1, tiled=True)  33.1 us
    dot_general x2, matrix products, per_device(): col_term = col_term + jnp.dot(vectors_part, loss_grad, precision=highest)  24.1 us
    all_gather x1, blocking collectives, per_device(): col_mass = jnp.sum(lax.all_gather(col_part, 'row'), axis=0)  23.7 us
    dot_general x2, matrix products, per_device(): lax.dot_general(col_block, loss_grad, (((1,), (1,)), ((), ())), precision...  17.4 us
  transfers between devices with their start and end apart: 5, of which 3 were waited for; matrix products, arithmetic and copies ran while one was open for 18% of the time, Pallas kernels for 0%

profile of v1, /device:TPU:2, one launch (start us, length us, event | category | flops | bytes accessed | tf_op | source)
XLA Modules:
  0.0 483.2 jit_solution(10882340301369968032)
XLA Ops:
  7.2 0.0 all-gather.4.cloned.1.call-start
  7.2 0.7 all-gather.4.cloned.1.call-update
  7.9 0.0 all-gather.6.cloned.1.call-start
  7.9 0.7 all-gather.6.cloned.1.call-update
  8.7 0.0 copy-start.9
  8.7 0.0 copy-start.8
  8.7 1.8 copy.27
  10.5 33.1 %all_to_all.10 = f32[8,32,2,8,128]{4,3,2,0,1:T(8,128)S(1)} all-to-all(f32[8,32,2,8,128]{4,3,2,0,1:T(8,128)S(1)} %bitcast.54), channel_id=1, replica_groups=mesh['row'=32,'col'=8] {'row'}, dimensions={1} | all-to-all | bytes 4194304 | tf_op jit(solution)/shard_map/all_to_all | solution.py:15
  43.6 1.5 copy.19
  45.1 8.5 %all-to-all-start.1 = ((f32[8,32,2,8,128]{4,3,2,1,0:T(8,128)}), f32[8,32,2,8,128]{4,3,2,1,0:T(8,128)S(1)}, u32[]{:S(2)}, u32[]{:S(2)}) async-start(f32[8,32,2,8,128]{4,3,2,1,0:T(8,128)} %copy.19), calls=%async_computation.1 | async-start | bytes 4194304 | tf_op jit(solution)/shard_map/all_to_all | solution.py:14
  53.6 0.0 reduce-scatter.3.cloned.1.call-start
  53.6 0.0 copy-done.9
  53.7 0.1 iota_compare_fusion
  53.8 0.1 lt.23
  53.9 0.0 copy-done.8
  53.9 0.1 copy.17
  54.1 0.1 squeeze.6
  54.2 51.8 %all-to-all-done.1 = f32[8,32,2,8,128]{4,3,2,1,0:T(8,128)S(1)} async-done(((f32[8,32,2,8,128]{4,3,2,1,0:T(8,128)}), f32[8,32,2,8,128]{4,3,2,1,0:T(8,128)S(1)}, u32[]{:S(2)}, u32[]{:S(2)}) %all-to-all-start.1) | async-done | bytes 2097184 | tf_op jit(solution)/shard_map/all_to_all | solution.py:14
  106.0 11.9 %scatter_custom_fusion = f32[4097,1024]{1,0:T(8,128)} fusion(s32[512]{0:T(512)S(1)} %bitcast.58, f32[]{:T(128)} %constant.7.clone.1, f32[64,8,8,128]{3,2,1,0:T(8,128)S(1)} %bitcast.55), kind=kCustom, calls=%fused_computation.12 | custom fusion | flops 524288 | bytes 18878468 | tf_op jit(solution)/shard_map/scatter-add | solution.py:33
  117.9 13.3 %slice_reduce_fusion = (f32[]{:T(128)}, f32[512,8,8,128]{3,1,2,0:T(8,128)}) fusion(f32[4097,1024]{1,0:T(8,128)} %scatter_custom_fusion), kind=kLoop, calls=%fused_computation.2 | loop fusion | flops 4194303 | bytes 33554436 | tf_op jit(solution)/shard_map/reduce_sum | solution.py:45
  131.2 72.8 %psum.14 = f32[]{:T(128)} all-reduce(f32[]{:T(128)} %get-tuple-element.10), channel_id=1, replica_groups=mesh['row'=32,'col'=8] {'row','col'}, use_global_device_ids=true, to_apply=%region_2.3 | all-reduce | flops 1 | bytes 8 | tf_op jit(solution)/shard_map/psum | solution.py:45
  204.7 14.3 %copy.21 = f32[512,8,8,128]{3,2,1,0:T(8,128)} copy(f32[512,8,8,128]{3,1,2,0:T(8,128)} %get-tuple-element.11) | data formatting | bytes 33554432
  218.9 7.2 %fusion.27 = (f32[32,128]{1,0:T(8,128)S(1)}, f32[128,8]{1,0:T(8,128)S(1)}) fusion(f32[128,32,8,128]{3,2,1,0:T(8,128)} %bitcast.52), kind=kLoop, calls=%fused_computation.53 | loop fusion | flops 8383488 | bytes 16797696 | tf_op jit(solution)/shard_map/reduce_sum | solution.py:42
  226.1 0.1 reduce_sum.42
  226.2 16.2 %psum.15 = f32[1024]{0:T(1024)S(1)} all-reduce(f32[1024]{0:T(1024)S(1)} %reduce_sum.42), channel_id=1, replica_groups=mesh['row'=32,'col'=8] {'col'}, use_global_device_ids=true, to_apply=%region_6.7 | all-reduce | flops 1024 | bytes 8192 | tf_op jit(solution)/shard_map/psum | solution.py:44
  242.5 23.7 %all-gather = f32[32,1,4096]{2,1,0:T(1,128)S(1)} all-gather(f32[1,1,4096]{2,1,0:T(1,128)S(1)} %bitcast.56), channel_id=1, replica_groups=mesh['row'=32,'col'=8] {'row'}, dimensions={0}, use_global_device_ids=true | all-gather | bytes 540672 | tf_op jit(solution)/shard_map/all_gather | solution.py:43
  266.1 0.4 reduce_sum.40
  266.5 11.7 %bitcast_bitcast_fusion = f32[128,8,32,128]{3,1,2,0:T(8,128)} fusion(f32[128,32,8,128]{3,2,1,0:T(8,128)} %bitcast.53), kind=kLoop, calls=%fused_computation.1 | loop fusion | bytes 33554432 | tf_op jit(solution)/shard_map/transpose | solution.py:38
  278.2 0.0 all-gather.4.cloned.1.call-done
  278.2 0.0 all-gather.6.cloned.1.call-done
  278.2 0.0 copy-start.2
  278.2 0.0 copy-start.3
  278.2 21.9 %fusion.5 = f32[512,4096]{1,0:T(8,128)S(1)} fusion(f32[128,8,32,128]{3,1,2,0:T(8,128)} %bitcast_bitcast_fusion, f32[512]{0:T(512)S(1)} %get-tuple-element.13, f32[4096]{0:T(1024)S(1)} %log_subtract_fusion, f32[300,4096]{1,0:T(8,128)} %all-gather.6.cloned.1.call-done, f32[300,1024]{1,0:T(8,128)} %all-gather.4.cloned.1.call-done), kind=kOutput, calls=%fused_computation.17 | convolution fusion | flops 7579107328 | bytes 22398976 | tf_op jit(solution)/shard_map/dot_general | solution.py:59
  300.1 0.0 copy-start
  300.2 0.0 copy-done.2
  300.2 0.0 copy-done.3
  300.2 25.7 %fusion.3 = f32[512,4096]{1,0:T(8,128)S(1)} fusion(f32[128,8,32,128]{3,1,2,0:T(8,128)} %bitcast_bitcast_fusion, f32[512]{0:T(512)S(1)} %get-tuple-element.12, f32[4096]{0:T(1024)S(1)} %log_subtract_fusion, f32[300,4096]{1,0:T(8,128)S(1)} %copy-done.2, f32[300,1024]{1,0:T(8,128)S(1)} %copy-done.3), kind=kOutput, calls=%fused_computation.15 | convolution fusion | flops 7579107328 | bytes 22398976 | tf_op jit(solution)/shard_map/dot_general | solution.py:59
  325.9 0.0 copy-start.1
  325.9 8.6 %convolution_bitcast_fusion.1 = f32[300,512]{1,0:T(8,128)S(1)} fusion(f32[512,4096]{1,0:T(8,128)S(1)} %fusion.3, f32[300,4096]{1,0:T(8,128)S(1)} %copy-done.2), kind=kOutput, calls=%fused_computation.38 | convolution fusion | flops 7549747200 | bytes 13918208 | tf_op jit(solution)/shard_map/dot_general | solution.py:73
  334.5 0.0 copy-done
  334.5 0.0 copy-done.1
  334.5 8.8 %convolution_bitcast_fusion = f32[300,512]{1,0:T(8,128)S(1)} fusion(f32[512,4096]{1,0:T(8,128)S(1)} %fusion.5, f32[300,4096]{1,0:T(8,128)S(1)} %copy-done.2), kind=kOutput, calls=%fused_computation.37 | convolution fusion | flops 7549747200 | bytes 13918208 | tf_op jit(solution)/shard_map/dot_general | solution.py:73
  343.3 1.1 pad_maximum_fusion
  344.4 0.0 reduce-scatter.3.cloned.1.call-update
  344.5 0.0 reduce-scatter.5.cloned.1.call-start
  344.5 11.3 %fusion.23 = f32[4096,300]{0,1:T(8,128)S(1)} fusion(f32[512,4096]{1,0:T(8,128)} %copy-done.1, f32[300,1024]{1,0:T(8,128)S(1)} %copy-done.3), kind=kOutput, calls=%fused_computation.42 | convolution fusion | flops 7549747200 | bytes 13926400 | tf_op jit(solution)/shard_map/dot_general | solution.py:75
  355.8 0.0 copy-start.4
  355.8 0.0 copy-start.6
  355.8 0.0 copy-start.5
  355.8 0.0 copy-start.7
  355.8 12.8 %fusion.18 = f32[300,4096]{1,0:T(8,128)} fusion(f32[4096,300]{0,1:T(8,128)S(1)} %fusion.23, f32[512,4096]{1,0:T(8,128)} %copy-done, f32[300,1024]{1,0:T(8,128)S(1)} %copy-done.3), kind=kOutput, calls=%fused_computation.33 | convolution fusion | flops 7550976000 | bytes 18907136 | tf_op jit(solution)/shard_map/dot_general | solution.py:75
  368.6 0.0 reduce-scatter.5.cloned.1.call-update
  368.6 11.2 %reduce-scatter.3.cloned.1.call-done = f32[300,128]{1,0:T(8,128)} async-done(((f32[300,1024]{1,0:T(8,128)}), f32[300,128]{1,0:T(8,128)}) %reduce-scatter.3.cloned.1.call-update) | async-done | bytes 153616 | tf_op jit(solution)/shard_map/reduce_scatter | solution.py:77
  379.9 0.0 copy-done.4
  379.9 0.0 copy-done.6
  379.9 1.7 multiply_subtract_fusion.1
  381.5 93.3 %reduce-scatter.5.cloned.1.call-done = f32[300,128]{1,0:T(8,128)} async-done(((f32[300,4096]{1,0:T(8,128)}), f32[300,128]{1,0:T(8,128)}) %reduce-scatter.5.cloned.1.call-update) | async-done | bytes 153616 | tf_op jit(solution)/shard_map/reduce_scatter | solution.py:78
  474.9 0.0 copy-done.5
  474.9 0.0 copy-done.7
  474.9 1.7 multiply_subtract_fusion
  (4 shorter events, 0.0 us)
Async XLA Ops:
  7.2 271.0 %all-gather.4.cloned.1.call-start = ((), (), s32[]{:S(2)}) async-start(), calls=%async_computation.4 | async-start | bytes 1400832 | tf_op jit(solution)/shard_map/all_gather | solution.py:46
  7.9 270.3 %all-gather.6.cloned.1.call-start = ((), (), s32[]{:S(2)}) async-start(), calls=%async_computation.5 | async-start | bytes 5136384 | tf_op jit(solution)/shard_map/all_gather | solution.py:47
  8.7 45.0 %copy-start.9 = (s32[1,1,8,32]{3,2,1,0:T(8,128)S(1)}, s32[1,1,8,32]{3,2,1,0:T(8,128)}, u32[]{:S(2)}) copy-start(s32[1,1,8,32]{3,2,1,0:T(8,128)} %param.9) | copy-start | bytes 3076
  8.7 45.3 %copy-start.8 = (s32[1,1,8,32,2]{3,4,2,1,0:T(2,128)S(1)}, s32[1,1,8,32,2]{3,4,2,1,0:T(2,128)}, u32[]{:S(2)}) copy-start(s32[1,1,8,32,2]{3,4,2,1,0:T(2,128)} %param.8) | copy-start | bytes 6148
  45.1 60.9 %all-to-all-start.1 = ((f32[8,32,2,8,128]{4,3,2,1,0:T(8,128)}), f32[8,32,2,8,128]{4,3,2,1,0:T(8,128)S(1)}, u32[]{:S(2)}, u32[]{:S(2)}) async-start(f32[8,32,2,8,128]{4,3,2,1,0:T(8,128)} %copy.19), calls=%async_computation.1 | async-start | bytes 4194304 | tf_op jit(solution)/shard_map/all_to_all | solution.py:14
  53.6 326.3 %reduce-scatter.3.cloned.1.call-start = ((), (), s32[]{:S(2)}) async-start(), calls=%async_computation.6 | async-start | bytes 1400832 | tf_op jit(solution)/shard_map/reduce_scatter | solution.py:77
  278.2 22.0 %copy-start.2 = (f32[300,4096]{1,0:T(8,128)S(1)}, f32[300,4096]{1,0:T(8,128)}, u32[]{:S(2)}) copy-start(f32[300,4096]{1,0:T(8,128)} %all-gather.6.cloned.1.call-done) | copy-start | bytes 14745604
  278.2 22.0 %copy-start.3 = (f32[300,1024]{1,0:T(8,128)S(1)}, f32[300,1024]{1,0:T(8,128)}, u32[]{:S(2)}) copy-start(f32[300,1024]{1,0:T(8,128)} %all-gather.4.cloned.1.call-done) | copy-start | bytes 3686404
  300.1 34.3 %copy-start = (f32[512,4096]{1,0:T(8,128)}, f32[512,4096]{1,0:T(8,128)S(1)}, u32[]{:S(2)}) copy-start(f32[512,4096]{1,0:T(8,128)S(1)} %fusion.5) | copy-start | bytes 25165828
  325.9 8.6 %copy-start.1 = (f32[512,4096]{1,0:T(8,128)}, f32[512,4096]{1,0:T(8,128)S(1)}, u32[]{:S(2)}) copy-start(f32[512,4096]{1,0:T(8,128)S(1)} %fusion.3) | copy-start | bytes 25165828
  344.5 130.4 %reduce-scatter.5.cloned.1.call-start = ((), (), s32[]{:S(2)}) async-start(), calls=%async_computation.7 | async-start | bytes 5136384 | tf_op jit(solution)/shard_map/reduce_scatter | solution.py:78
  355.8 24.1 %copy-start.4 = (f32[300,128]{1,0:T(8,128)S(1)}, f32[300,128]{1,0:T(8,128)}, u32[]{:S(2)}) copy-start(f32[300,128]{1,0:T(8,128)} %param.10) | copy-start | bytes 460804
  355.8 24.1 %copy-start.6 = (f32[300,128]{1,0:T(8,128)S(1)}, f32[300,128]{1,0:T(8,128)}, u32[]{:S(2)}) copy-start(f32[300,128]{1,0:T(8,128)} %param.12) | copy-start | bytes 460804
  355.8 119.1 %copy-start.5 = (f32[300,128]{1,0:T(8,128)S(1)}, f32[300,128]{1,0:T(8,128)}, u32[]{:S(2)}) copy-start(f32[300,128]{1,0:T(8,128)} %param.11) | copy-start | bytes 460804
  355.8 119.1 %copy-start.7 = (f32[300,128]{1,0:T(8,128)S(1)}, f32[300,128]{1,0:T(8,128)}, u32[]{:S(2)}) copy-start(f32[300,128]{1,0:T(8,128)} %param.13) | copy-start | bytes 460804
Sparse Core Ops, SparseCore 0:
  9.7 44.0 all-gather.3
  56.2 54.9 all-gather.5
  344.6 35.2 reduce-scatter.2
  383.8 91.0 reduce-scatter.4
